TPU v7x, 128 devices: a whole 4x4x4 slice. The times are simulated.
128 devices in a mesh: blk: 32 (over y_hi, x, z), head: 4 (over y_lo, core).
Axes of the slice: x: 4, y: 4 (y_hi: 2, y_lo: 2; y = y_hi * 2 + y_lo), z: 4, core: 2. Of those that a mesh axis runs over, the one named last changes fastest.
Arguments:
- states_in: bfloat16 [8192, 2048], P('blk'), may hold values from -12 to 12
- w_qkv: bfloat16 [3, 2048, 2048], P(None, None, 'head'), may hold values from -0.35355339 to 0.35355339
- qk_gain: float32 [2, 2048], P(None, 'head'), may hold values from 0.8 to 7.8
- w_out: bfloat16 [2048, 2048], P('head'), may hold values from -0.125 to 0.125
- post_gain: float32 [2, 2048], replicated, may hold values from 0.5 to 1.5
- w_gate_up: bfloat16 [2, 2048, 8192], P(None, None, 'blk'), may hold values from -0.125 to 0.125
- w_down: bfloat16 [8192, 2048], P('blk'), may hold values from -0.0625 to 0.0625
- cache_keys: bfloat16 [32, 256, 2048], P('blk', None, 'head'), may hold values from -6 to 6
- cache_values: bfloat16 [32, 256, 2048], P('blk', None, 'head'), may hold values from -6 to 6
- slot_node: int32 [32], replicated, may hold values from 0 to 31, each once
- node_length: int32 [32], replicated, may hold values from 1 to 256, 5120 in all
- node_parent: int32 [28], replicated, may hold values from 0 to 3
- leaf_segment: int32 [32, 256], replicated, may hold values from 0 to 7, never falling along the last dimension, each value on 1 to 128 neighbouring positions
- leaf_node: int32 [32, 8], replicated, may hold values from 4 to 31
Outputs:
- layer_out: bfloat16 [8192, 2048], P(('blk', 'head'))
Inputs may be any that keep to these rules, and one draw needn't show every extreme that they name: Slot s holds node slot_node[s]; every node is held once. Rows 0 to node_length[n] - 1 of node n's slot are valid; the longest node has 256 rows. Nodes 0 to 3 are roots; middle node 4 + i hangs under root node_parent[i]. `leaf_segment`: never falls along a group; every leaf of a group has 1 to 128 tokens. `leaf_node`: every leaf hangs under a middle node.
All inputs are finite; a program needn't handle non-finite values.
Results may differ from a plain program's by a relative error of at most 0.025.
Values may be sent and summed in bfloat16 or wider, within the bound.
No kernel may reach another device: no remote copies, remote signals or barrier semaphores. Data moves between devices by JAX's collectives and lax.ppermute only.
A program may use at most 192 MiB of HBM per device.

v0:
```python
import jax
import jax.numpy as jnp
from jax import lax
from jax.sharding import PartitionSpec as P

HD = 128
EPS = 1e-06
THETA = 500000.0
NEG = -1e30


def tree_info(leaf_segment, leaf_node, node_parent, node_length):
    groups, tok_rows = leaf_segment.shape
    leaf_count = leaf_node.shape[1]
    middles = node_parent.shape[0]
    all_nodes = node_length.shape[0]
    tenant_count = all_nodes - middles
    leaf_ids = jnp.arange(leaf_count, dtype=jnp.int32)
    onehot = (leaf_segment[:, :, None] == leaf_ids[None, None, :]).astype(jnp.int32)
    middle = jnp.sum(onehot * leaf_node[:, None, :], axis=-1)
    counts = jnp.sum(onehot, axis=1)
    starts = jnp.cumsum(counts, axis=1) - counts
    first_at = jnp.sum(onehot * starts[:, None, :], axis=-1)
    middle_ids = jnp.arange(middles, dtype=jnp.int32) + tenant_count
    root_node = jnp.sum(jnp.where(middle[..., None] == middle_ids, node_parent, 0), axis=-1)
    node_ids = jnp.arange(all_nodes, dtype=jnp.int32)
    len_middle = jnp.sum(jnp.where(middle[..., None] == node_ids, node_length, 0), axis=-1)
    len_root = jnp.sum(jnp.where(root_node[..., None] == node_ids, node_length, 0), axis=-1)
    offsets = jnp.arange(tok_rows, dtype=jnp.int32)[None, :] - first_at
    position = len_root + len_middle + offsets
    return (middle, root_node, position)


def rotate(values_in, position):
    half_size = values_in.shape[-1] // 2
    frequency = THETA ** (-2.0 * jnp.arange(half_size, dtype=jnp.float32) / values_in.shape[-1])
    angles = position.astype(jnp.float32)[:, None] * frequency[None, :]
    cosine = jnp.cos(angles)[:, None, :]
    sine_part = jnp.sin(angles)[:, None, :]
    lower = values_in[..., :half_size]
    upper = values_in[..., half_size:]
    return jnp.concatenate(
        [lower * cosine - upper * sine_part, upper * cosine + lower * sine_part], axis=-1
    )


def rms_norm(values_in, gain):
    return (
        values_in * lax.rsqrt(jnp.mean(values_in * values_in, axis=-1, keepdims=True) + EPS) * gain
    )


def lookup_length(nodes, node_length):
    node_ids = jnp.arange(node_length.shape[0], dtype=jnp.int32)
    return jnp.sum(jnp.where(nodes[:, None] == node_ids[None, :], node_length[None, :], 0), axis=-1)


def masked_partial(scores, visible, values_in):
    masked = jnp.where(visible, scores, NEG)
    peak = jnp.max(masked, axis=-1)
    weights = jnp.where(visible, jnp.exp(masked - peak[..., None]), 0.0)
    totals = jnp.sum(weights, axis=-1)
    summed = jnp.einsum(
        "rhk,khe->rhe", weights.astype(jnp.bfloat16), values_in, preferred_element_type=jnp.float32
    )
    return (peak, totals, summed)


def combine(left, right):
    peak = jnp.maximum(left[0], right[0])
    scale_left = jnp.exp(left[0] - peak)
    scale_right = jnp.exp(right[0] - peak)
    totals = left[1] * scale_left + right[1] * scale_right
    summed = left[2] * scale_left[..., None] + right[2] * scale_right[..., None]
    return (peak, totals, summed)


def cache_partial(queries, middle, root_node, keys_in, values_in, nodes, lengths):
    slots, node_rows, columns = keys_in.shape
    head_count, size = (queries.shape[1], queries.shape[2])
    flat_keys = keys_in.reshape(slots * node_rows, head_count, size)
    flat_values = values_in.reshape(slots * node_rows, head_count, size)
    node_flat = jnp.broadcast_to(nodes[:, None], (slots, node_rows)).reshape(-1)
    length_flat = jnp.broadcast_to(lengths[:, None], (slots, node_rows)).reshape(-1)
    row_flat = jnp.broadcast_to(
        jnp.arange(node_rows, dtype=jnp.int32)[None, :], (slots, node_rows)
    ).reshape(-1)
    visible = (
        (node_flat[None, :] == middle[:, None]) | (node_flat[None, :] == root_node[:, None])
    ) & (row_flat < length_flat)[None, :]
    scores = jnp.einsum(
        "rhe,khe->rhk", queries, flat_keys, preferred_element_type=jnp.float32
    ) * size ** (-0.5)
    return masked_partial(scores, visible[:, None, :], flat_values)


def on_device(
    states_in,
    w_qkv,
    qk_gain,
    w_out,
    post_gain,
    w_gate_up,
    w_down,
    cache_keys,
    cache_values,
    slot_node,
    node_length,
    node_parent,
    leaf_segment,
    leaf_node,
):
    blk_index = lax.axis_index("blk")
    head_index = lax.axis_index("head")
    head_devices = lax.axis_size("head")
    tok_rows = states_in.shape[0]
    heads_here = w_qkv.shape[2] // HD
    columns = w_qkv.shape[2] * head_devices
    qkv_raw = jnp.einsum("td,cdw->ctw", states_in, w_qkv, preferred_element_type=jnp.float32)
    query_squares, key_squares = lax.psum(
        (jnp.sum(qkv_raw[0] * qkv_raw[0], axis=1), jnp.sum(qkv_raw[1] * qkv_raw[1], axis=1)), "head"
    )
    middle_all, root_all, position_all = tree_info(
        leaf_segment, leaf_node, node_parent, node_length
    )
    position = lax.dynamic_index_in_dim(position_all, blk_index, 0, keepdims=False)
    middle_own = lax.dynamic_index_in_dim(middle_all, blk_index, 0, keepdims=False)
    root_own = lax.dynamic_index_in_dim(root_all, blk_index, 0, keepdims=False)
    segment_own = lax.dynamic_index_in_dim(leaf_segment, blk_index, 0, keepdims=False)

    def normed(raw_part, squares, gain):
        scaled = raw_part * lax.rsqrt(squares / columns + EPS)[:, None] * gain
        return rotate(scaled.reshape(tok_rows, heads_here, HD), position).astype(jnp.bfloat16)

    queries = normed(qkv_raw[0], query_squares, qk_gain[0])
    keys_new = normed(qkv_raw[1], key_squares, qk_gain[1])
    values_cast = qkv_raw[2].astype(jnp.bfloat16).reshape(tok_rows, heads_here, HD)
    order = jnp.arange(tok_rows, dtype=jnp.int32)
    see_leaf = (segment_own[:, None] == segment_own[None, :]) & (order[None, :] <= order[:, None])
    leaf_scores = jnp.einsum(
        "rhe,khe->rhk", queries, keys_new, preferred_element_type=jnp.float32
    ) * HD ** (-0.5)
    local_state = masked_partial(leaf_scores, see_leaf[:, None, :], values_cast)
    keys_piece = lax.all_gather(cache_keys, "blk", axis=0, tiled=True)
    values_piece = lax.all_gather(cache_values, "blk", axis=0, tiled=True)
    lengths = lookup_length(slot_node, node_length)
    needed = jnp.any(
        (slot_node[:, None] == middle_own[None, :]) | (slot_node[:, None] == root_own[None, :])
    )

    def attend(carry):
        return combine(
            carry,
            cache_partial(
                queries, middle_own, root_own, keys_piece, values_piece, slot_node, lengths
            ),
        )

    def keep(carry):
        return carry

    state = lax.cond(needed, attend, keep, local_state)
    attended = (
        (state[2] / state[1][..., None]).astype(jnp.bfloat16).reshape(tok_rows, heads_here * HD)
    )
    attn_part = jnp.dot(attended, w_out, preferred_element_type=jnp.float32)
    own_rows = tok_rows // head_devices
    attn_whole = lax.psum(attn_part.astype(jnp.bfloat16), "head").astype(jnp.float32)
    attn_proj = lax.dynamic_slice_in_dim(attn_whole, head_index * own_rows, own_rows, 0)
    state_rows = lax.dynamic_slice_in_dim(states_in, head_index * own_rows, own_rows, 0)
    mid_state = (state_rows.astype(jnp.float32) + rms_norm(attn_proj, post_gain[0])).astype(
        jnp.bfloat16
    )
    gate_up = jnp.einsum(
        "rd,cdf->crf",
        lax.all_gather(mid_state, "blk", axis=0, tiled=True),
        w_gate_up,
        preferred_element_type=jnp.float32,
    )
    hidden = (jax.nn.silu(gate_up[0]) * gate_up[1]).astype(jnp.bfloat16)
    mlp_proj = lax.psum_scatter(
        jnp.dot(hidden, w_down, preferred_element_type=jnp.float32).astype(jnp.bfloat16),
        "blk",
        scatter_dimension=0,
        tiled=True,
    ).astype(jnp.float32)
    return (mid_state.astype(jnp.float32) + rms_norm(mlp_proj, post_gain[1])).astype(jnp.bfloat16)


def solution(mesh):
    placed = (
        P("blk", None),
        P(None, None, "head"),
        P(None, "head"),
        P("head", None),
        P(),
        P(None, None, "blk"),
        P("blk", None),
        P("blk", None, "head"),
        P("blk", None, "head"),
        P(),
        P(),
        P(),
        P(),
        P(),
    )
    return jax.shard_map(
        on_device, mesh=mesh, in_specs=placed, out_specs=P(("blk", "head"), None), check_vma=False
    )
```

profile of v0, /device:TPU:0, one launch (start us, length us, event | category | flops | bytes accessed | tf_op | source)
XLA Modules:
  0.0 681.2 jit_solution(14530980794366099243)
XLA Ops:
  6.5 0.0 copy-start
  6.5 0.0 all-gather.4.cloned.1.call-start
  6.6 0.7 all-gather.4.cloned.1.call-update
  7.3 0.0 copy-start.5
  7.3 0.0 all-gather.6.cloned.1.call-start
  7.3 0.7 all-gather.6.cloned.1.call-update
  8.0 0.0 all-reduce.3.cloned.1.call-start
  8.1 1.4 convert_reduce_fusion
  9.5 0.2 reduce_window_sum.11
  9.6 0.8 copy.50
  10.4 4.9 convolution_bitcast_fusion
  15.4 0.1 multiply_reduce_fusion.1
  15.5 1.0 copy.53
  16.5 0.2 copy.52
  16.7 0.0 copy-done.2
  16.7 0.2 select_reduce_fusion.4
  17.0 0.0 copy-done.7
  17.0 0.2 select_reduce_fusion.3
  17.2 0.0 copy-done.4
  17.2 0.7 or_reduce_fusion
  18.5 7.1 %all-reduce = (f32[256]{0:T(256)S(1)}, f32[256]{0:T(256)S(1)}) all-reduce(f32[256]{0:T(256)S(1)} %get-tuple-element.109, f32[256]{0:T(256)S(1)} %get-tuple-element.108), channel_id=1, replica_groups=mesh['blk'=32,'head'=4] {'head'}, use_global_device_ids=true, to_apply=%region_11.12 | all-reduce | flops 512 | bytes 4096 | tf_op jit(solution)/shard_map/psum | solution.py:120
  25.6 0.0 copy-done.6
  25.6 0.6 select_reduce_fusion.2
  26.3 0.0 copy-done.5
  26.3 0.5 multiply_cosine_fusion
  26.9 1.1 multiply_multiply_fusion
  28.0 0.1 multiply_multiply_fusion.1
  28.1 0.4 subtract_convert_fusion.1
  28.6 0.1 pad_maximum_fusion
  28.7 0.1 fusion.58
  28.8 0.4 fusion.70
  29.2 0.2 fusion.42
  29.4 0.3 convolution_bitcast_fusion.1
  29.8 87.6 %all-gather.4.cloned.1.call-done = bf16[32,256,512]{2,1,0:T(8,128)(2,1)} async-done(((bf16[1,256,512]{2,1,0:T(8,128)(2,1)}), bf16[32,256,512]{2,1,0:T(8,128)(2,1)}) %all-gather.4.cloned.1.call-update) | async-done | bytes 8388624 | tf_op jit(solution)/shard_map/all_gather | solution.py:144
  117.3 105.1 %all-gather.6.cloned.1.call-done = bf16[32,256,512]{2,1,0:T(8,128)(2,1)} async-done(((bf16[1,256,512]{2,1,0:T(8,128)(2,1)}), bf16[32,256,512]{2,1,0:T(8,128)(2,1)}) %all-gather.6.cloned.1.call-update) | async-done | bytes 8388624 | tf_op jit(solution)/shard_map/all_gather | solution.py:145
  222.5 84.2 %conditional.1 = ((f32[256,4]{0,1:T(4,128)S(1)}, f32[256,4,128]{0,2,1:T(8,128)S(1)})) conditional(s32[]{:T(128)} %convert_element_type.61, (f32[256,4]{0,1:T(4,128)S(1)}, f32[256,4,128]{0,2,1:T(8,128)S(1)}) %tuple.12, (s32[32]{0:T(128)S(1)}, s32[256]{0:T(256)S(1)}, s32[256]{0:T(256)S(1)}, s32[32,32]{1,0:T(8,128)S(1)}, s32[32]{0:T(128)S(1)}, ...), branch_computations={%region_14.15_spmd, %region_15.19_spmd} | conditional | flops 4412816384 | bytes 163015328 | solution.py:162
  222.5 0.1 broadcast_bitcast_fusion
  222.6 0.2 select_reduce_fusion
  222.7 0.1 iota_compare_fusion
  222.9 6.9 %or_and_fusion = pred[256,8192]{0,1:T(8,128)(4,1)} fusion(s32[256]{0:T(256)S(1)} %get-tuple-element.44, s32[256]{0:T(256)S(1)} %get-tuple-element.43, s32[8192]{0:T(1024)S(1)} %bitcast.80, pred[8192]{0:T(1024)(128)(4,1)S(1)} %lt.18), kind=kLoop, calls=%fused_computation.10 | loop fusion | flops 8388608 | bytes 2140160 | tf_op jit(solution)/shard_map/cond/branch_1_fun/and | solution.py:88
  229.7 12.5 %reshape.255 = bf16[8192,4,128]{2,1,0:T(4,128)(2,1)} reshape(bf16[32,256,512]{2,1,0:T(8,128)(2,1)} %get-tuple-element.47) | data formatting | bytes 16777216 | tf_op jit(solution)/shard_map/cond/branch_1_fun/reshape | solution.py:81
  242.2 16.4 %fusion = (f32[256,4]{0,1:T(4,128)S(1)}, f32[4,8192,256]{2,1,0:T(8,128)}) fusion(pred[256,8192]{0,1:T(8,128)(4,1)} %or_and_fusion, bf16[256,4,128]{2,0,1:T(8,128)(2,1)S(1)} %get-tuple-element.48, bf16[8192,4,128]{2,1,0:T(4,128)(2,1)} %reshape.255), kind=kOutput, calls=%fused_computation.2 | convolution fusion | flops 2172648448 | bytes 44306432 | tf_op jit(solution)/shard_map/cond/branch_1_fun/rhe,khe->rhk/dot_general | solution.py:91
  258.6 15.1 %fusion.2 = f32[256,4]{0,1:T(4,128)S(1)} fusion(f32[4,8192,256]{2,1,0:T(8,128)} %get-tuple-element.120, f32[256,4]{0,1:T(4,128)S(1)} %get-tuple-element.119, pred[256,8192]{0,1:T(8,128)(4,1)} %or_and_fusion), kind=kLoop, calls=%fused_computation.4 | loop fusion | flops 41942016 | bytes 35659776 | tf_op jit(solution)/shard_map/cond/branch_1_fun/reduce_sum | solution.py:62
  273.8 12.5 %reshape.256 = bf16[8192,4,128]{2,1,0:T(4,128)(2,1)} reshape(bf16[32,256,512]{2,1,0:T(8,128)(2,1)} %get-tuple-element.50) | data formatting | bytes 16777216 | tf_op jit(solution)/shard_map/cond/branch_1_fun/reshape | solution.py:82
  286.3 1.0 copy.56
  287.3 19.1 %fusion.19 = f32[256,4,128]{2,0,1:T(8,128)S(1)} fusion(bf16[8192,4,128]{2,1,0:T(4,128)(2,1)} %reshape.256, f32[4,8192,256]{2,1,0:T(8,128)} %get-tuple-element.120, f32[256,4]{0,1:T(4,128)S(1)} %get-tuple-element.119, pred[256,8192]{0,1:T(8,128)(4,1)} %or_and_fusion, f32[256,4,128]{2,0,1:T(8,128)} %copy.56, f32[256,4]{0,1:T(4,128)S(1)} %get-tuple-element.118, ...), kind=kOutput, calls=%fused_computation.13 | convolution fusion | flops 2189819904 | bytes 45101056 | tf_op jit(solution)/shard_map/cond/branch_1_fun/rhk,khe->rhe/dot_general | solution.py:63
  306.4 0.2 copy.62
  306.7 3.4 convolution_convert_fusion.1
  310.1 0.0 all-reduce.3.cloned.1.call-update
  310.1 0.0 all-gather.8.cloned.1.call-start
  310.2 39.3 %all-reduce.3.cloned.1.call-done = bf16[256,2048]{1,0:T(8,128)(2,1)} async-done(((bf16[256,2048]{1,0:T(8,128)(2,1)}), bf16[256,2048]{1,0:T(8,128)(2,1)}) %all-reduce.3.cloned.1.call-update) | async-done | bytes 1048592 | tf_op jit(solution)/shard_map/psum | solution.py:168
  349.5 1.1 fusion.46
  350.6 1.9 fusion.45
  352.5 0.0 all-gather.8.cloned.1.call-update
  352.5 0.0 copy-start.8
  352.5 0.3 reduce-scatter.2.cloned.1.call-start
  352.8 105.4 %all-gather.8.cloned.1.call-done = bf16[2048,2048]{1,0:T(8,128)(2,1)} async-done(((bf16[64,2048]{1,0:T(8,128)(2,1)}), bf16[2048,2048]{1,0:T(8,128)(2,1)}) %all-gather.8.cloned.1.call-update) | async-done | bytes 8388624 | tf_op jit(solution)/shard_map/all_gather | solution.py:176
  458.2 0.0 copy-done
  458.2 6.9 %fusion.31 = f32[2,2048,256]{2,1,0:T(8,128)S(1)} fusion(bf16[2,2048,256]{2,1,0:T(8,128)(2,1)S(1)} %copy-done, bf16[2048,2048]{1,0:T(8,128)(2,1)} %all-gather.8.cloned.1.call-done), kind=kOutput, calls=%fused_computation.28 | convolution fusion | flops 4294967296 | bytes 14680064 | tf_op jit(solution)/shard_map/rd,cdf->crf/dot_general | solution.py:174
  465.1 5.7 convolution_convert_fusion
  470.7 0.0 reduce-scatter.2.cloned.1.call-update
  470.8 201.0 %reduce-scatter.2.cloned.1.call-done = bf16[64,2048]{1,0:T(8,128)(2,1)} async-done(((bf16[2048,2048]{1,0:T(8,128)(2,1)}), bf16[64,2048]{1,0:T(8,128)(2,1)}) %reduce-scatter.2.cloned.1.call-update) | async-done | bytes 262160 | tf_op jit(solution)/shard_map/reduce_scatter | solution.py:181
  671.7 1.1 fusion.47
  672.9 1.8 fusion.50
  (25 shorter events, 0.2 us)
Async XLA Ops:
  6.5 451.7 %copy-start = (bf16[2,2048,256]{2,1,0:T(8,128)(2,1)S(1)}, bf16[2,2048,256]{2,1,0:T(8,128)(2,1)}, u32[]{:S(2)}) copy-start(bf16[2,2048,256]{2,1,0:T(8,128)(2,1)} %param.21) | copy-start | bytes 6291460
  6.5 10.2 %copy-start.2 = (s32[32,256]{1,0:T(8,128)S(1)}, s32[32,256]{1,0:T(8,128)}, u32[]{:S(2)}) copy-start(s32[32,256]{1,0:T(8,128)} %param.28) | copy-start | bytes 98308
  6.5 10.4 %copy-start.7 = (s32[28]{0:T(128)S(1)}, s32[28]{0:T(128)}, u32[]{:S(2)}) copy-start(s32[28]{0:T(128)} %param.27) | copy-start | bytes 340
  6.5 10.6 %copy-start.4 = (s32[32]{0:T(128)S(1)}, s32[32]{0:T(128)}, u32[]{:S(2)}) copy-start(s32[32]{0:T(128)} %param.25) | copy-start | bytes 388
  6.5 19.1 %copy-start.6 = (s32[32]{0:T(128)S(1)}, s32[32]{0:T(128)}, u32[]{:S(2)}) copy-start(s32[32]{0:T(128)} %param.26) | copy-start | bytes 388
  6.5 110.8 %all-gather.4.cloned.1.call-start = ((), (), s32[]{:S(2)}) async-start(), calls=%async_computation.1 | async-start | bytes 8650752 | tf_op jit(solution)/shard_map/all_gather | solution.py:144
  7.3 19.0 %copy-start.5 = (f32[2,512]{1,0:T(2,128)S(1)}, f32[2,512]{1,0:T(2,128)}, u32[]{:S(2)}) copy-start(f32[2,512]{1,0:T(2,128)} %param.18) | copy-start | bytes 12292
  7.3 215.2 %all-gather.6.cloned.1.call-start = ((), (), s32[]{:S(2)}) async-start(), calls=%async_computation.2 | async-start | bytes 8650752 | tf_op jit(solution)/shard_map/all_gather | solution.py:145
  8.0 341.4 %all-reduce.3.cloned.1.call-start = ((), (), s32[]{:S(2)}) async-start(), calls=%async_computation.3 | async-start | bytes 2097152 | tf_op jit(solution)/shard_map/psum | solution.py:168
  222.5 87.7 %copy-start.3 = (f32[2,2048]{1,0:T(2,128)S(1)}, f32[2,2048]{1,0:T(2,128)}, u32[]{:S(2)}) copy-start(f32[2,2048]{1,0:T(2,128)} %param.20) | copy-start | bytes 49156
  310.1 148.1 %all-gather.8.cloned.1.call-start = ((), (), s32[]{:S(2)}) async-start(), calls=%async_computation.4 | async-start | bytes 8650752 | tf_op jit(solution)/shard_map/all_gather | solution.py:176
  352.5 112.5 %copy-start.8 = (bf16[256,2048]{1,0:T(8,128)(2,1)S(1)}, bf16[256,2048]{1,0:T(8,128)(2,1)}, u32[]{:S(2)}) copy-start(bf16[256,2048]{1,0:T(8,128)(2,1)} %param.22) | copy-start | bytes 3145732
  352.5 319.2 %reduce-scatter.2.cloned.1.call-start = ((), (), s32[]{:S(2)}) async-start(), calls=%async_computation.5 | async-start | bytes 8650752 | tf_op jit(solution)/shard_map/reduce_scatter | solution.py:181
  470.7 202.1 %copy-start.1 = (bf16[64,2048]{1,0:T(8,128)(2,1)S(1)}, bf16[64,2048]{1,0:T(8,128)(2,1)}, u32[]{:S(2)}) copy-start(bf16[64,2048]{1,0:T(8,128)(2,1)} %fusion.45) | copy-start | bytes 786436
Sparse Core Ops, SparseCore 0:
  10.5 106.7 all-gather.3
  120.4 101.9 all-gather.5
  310.2 39.2 all-reduce.2
  352.9 105.2 all-gather.7
  470.9 200.8 reduce-scatter.1
where the time goes:
time: 682 us; the launch traced here: 681 us
  waiting for transfers between devices  540 us (79%)
  matrix products  57 us (8%)
  other arithmetic  34.4 us (5%)
  local copies, waits for them, and re-layouts  28.5 us (4%)
  between operations  14.1 us (2%)
  blocking collectives  7.07 us (1%)
    reduce_scatter x1, waiting for transfers between devices, on_device(): lax.psum_scatter(jnp.dot(hidden, w_down, preferred_element_type=jnp.float...  201 us
    all_gather x1, waiting for transfers between devices, on_device(): lax.all_gather(mid_state, 'blk', axis=0, tiled=True)  105 us
    all_gather x1, waiting for transfers between devices, on_device(): values_piece = lax.all_gather(cache_values, 'blk', axis=0, tiled=True)  105 us
    all_gather x1, waiting for transfers between devices, on_device(): keys_piece = lax.all_gather(cache_keys, 'blk', axis=0, tiled=True)  87.6 us
    psum x1, waiting for transfers between devices, on_device(): lax.psum(attn_part.astype(jnp.bfloat16), 'head').astype(jnp.float32)  39.3 us
    dot_general x2, matrix products, masked_partial(): jnp.einsum('rhk,khe->rhe', weights.astype(jnp.bfloat16), values_in, prefe...  19.5 us
    dot_general x1, matrix products, cache_partial(): jnp.einsum('rhe,khe->rhk', queries, flat_keys, preferred_element_type=jnp...  16.4 us
    reduce_sum x2, other arithmetic, masked_partial(): totals = jnp.sum(weights, axis=-1)  15.3 us
  transfers between devices with their start and end apart: 5, of which 5 were waited for; matrix products, arithmetic and copies ran while one was open for 2% of the time, Pallas kernels for 0%

commit v1 on v0

--- a/solution.py
+++ b/solution.py
@@ -7,6 +7,13 @@
 EPS = 1e-06
 THETA = 500000.0
 NEG = -1e30
+
+
+def store_the_bands(matrix, named_axis="blk"):
+    prior = lax.all_to_all(
+        jnp.stack([matrix for _ in range(lax.axis_size(named_axis))], 0), named_axis, 0, 0
+    )
+    return jnp.concatenate(prior, axis=0)
 
 
 def tree_info(leaf_segment, leaf_node, node_parent, node_length):
@@ -172,10 +179,7 @@
         jnp.bfloat16
     )
     gate_up = jnp.einsum(
-        "rd,cdf->crf",
-        lax.all_gather(mid_state, "blk", axis=0, tiled=True),
-        w_gate_up,
-        preferred_element_type=jnp.float32,
+        "rd,cdf->crf", store_the_bands(mid_state), w_gate_up, preferred_element_type=jnp.float32
     )
     hidden = (jax.nn.silu(gate_up[0]) * gate_up[1]).astype(jnp.bfloat16)
     mlp_proj = lax.psum_scatter(

time: 682 us -> 687 us (level)
  blocking collectives: 7.07 us -> 115 us
  waiting for transfers between devices: 540 us -> 439 us
    all_to_all x0 -> x1, blocking collectives: none -> 108 us  [store_the_bands(): lax.all_to_all(jnp.stack([matrix for _ in range(lax.axis_size(named_axis)...]
    all_gather x1 -> x0, waiting for transfers between devices: 105 us -> none  [on_device(): lax.all_gather(mid_state, 'blk', axis=0, tiled=True)]
  transfers between devices with their start and end apart: 5 -> 4, of which waited for: 5 -> 4; matrix products, arithmetic and copies ran while one was open for 2% -> 2% of each run, Pallas kernels for 0% -> 0%
where the time goes in v1:
time: 687 us; the launch traced here: 685 us
  waiting for transfers between devices  439 us (64%)
  blocking collectives  115 us (17%)
  matrix products  54.7 us (8%)
  other arithmetic  33.7 us (5%)
  local copies, waits for them, and re-layouts  29.5 us (4%)
  between operations  14 us (2%)
    reduce_scatter x1, waiting for transfers between devices, on_device(): lax.psum_scatter(jnp.dot(hidden, w_down, preferred_element_type=jnp.float...  205 us
    all_to_all x1, blocking collectives, store_the_bands(): lax.all_to_all(jnp.stack([matrix for _ in range(lax.axis_size(named_axis)...  108 us
    all_gather x1, waiting for transfers between devices, on_device(): values_piece = lax.all_gather(cache_values, 'blk', axis=0, tiled=True)  105 us
    all_gather x1, waiting for transfers between devices, on_device(): keys_piece = lax.all_gather(cache_keys, 'blk', axis=0, tiled=True)  87.6 us
    psum x1, waiting for transfers between devices, on_device(): lax.psum(attn_part.astype(jnp.bfloat16), 'head').astype(jnp.float32)  39.3 us
    dot_general x2, matrix products, masked_partial(): jnp.einsum('rhk,khe->rhe', weights.astype(jnp.bfloat16), values_in, prefe...  19.5 us
    dot_general x1, matrix products, cache_partial(): jnp.einsum('rhe,khe->rhk', queries, flat_keys, preferred_element_type=jnp...  16.4 us
    reduce_sum x2, other arithmetic, masked_partial(): totals = jnp.sum(weights, axis=-1)  15.3 us
  transfers between devices with their start and end apart: 4, of which 4 were waited for; matrix products, arithmetic and copies ran while one was open for 2% of the time, Pallas kernels for 0%

profile of v1, /device:TPU:0, one launch (start us, length us, event | category | flops | bytes accessed | tf_op | source)
XLA Modules:
  0.0 685.5 jit_solution(989611545305038534)
XLA Ops:
  6.5 0.0 copy-start
  6.5 0.0 all-gather.3.cloned.1.call-start
  6.6 0.7 all-gather.3.cloned.1.call-update
  7.3 0.0 copy-start.4
  7.3 0.0 all-gather.5.cloned.1.call-start
  7.3 0.7 all-gather.5.cloned.1.call-update
  8.0 0.0 all-reduce.3.cloned.1.call-start
  8.1 1.4 convert_reduce_fusion
  9.5 0.2 reduce_window_sum.11
  9.6 0.8 copy.50
  10.4 4.9 convolution_bitcast_fusion.1
  15.4 0.1 multiply_reduce_fusion.1
  15.5 1.0 copy.53
  16.5 0.2 copy.52
  16.7 0.0 copy-done.1
  16.7 0.2 select_reduce_fusion.4
  17.0 0.0 copy-done.6
  17.0 0.2 select_reduce_fusion.3
  17.2 0.0 copy-done.3
  17.2 0.7 or_reduce_fusion
  18.5 7.1 %all-reduce = (f32[256]{0:T(256)S(1)}, f32[256]{0:T(256)S(1)}) all-reduce(f32[256]{0:T(256)S(1)} %get-tuple-element.109, f32[256]{0:T(256)S(1)} %get-tuple-element.108), channel_id=1, replica_groups=mesh['blk'=32,'head'=4] {'head'}, use_global_device_ids=true, to_apply=%region_11.12 | all-reduce | flops 512 | bytes 4096 | tf_op jit(solution)/shard_map/psum | solution.py:127
  25.6 0.0 copy-done.5
  25.6 0.6 select_reduce_fusion.2
  26.3 0.0 copy-done.4
  26.3 0.5 multiply_cosine_fusion
  26.9 1.1 multiply_multiply_fusion
  28.0 0.1 multiply_multiply_fusion.1
  28.1 0.4 subtract_convert_fusion.1
  28.6 0.1 pad_maximum_fusion
  28.7 0.1 fusion.53
  28.8 0.4 fusion.65
  29.2 0.2 fusion.37
  29.4 0.3 convolution_bitcast_fusion.2
  29.8 87.6 %all-gather.3.cloned.1.call-done = bf16[32,256,512]{2,1,0:T(8,128)(2,1)} async-done(((bf16[1,256,512]{2,1,0:T(8,128)(2,1)}), bf16[32,256,512]{2,1,0:T(8,128)(2,1)}) %all-gather.3.cloned.1.call-update) | async-done | bytes 8388624 | tf_op jit(solution)/shard_map/all_gather | solution.py:151
  117.3 105.1 %all-gather.5.cloned.1.call-done = bf16[32,256,512]{2,1,0:T(8,128)(2,1)} async-done(((bf16[1,256,512]{2,1,0:T(8,128)(2,1)}), bf16[32,256,512]{2,1,0:T(8,128)(2,1)}) %all-gather.5.cloned.1.call-update) | async-done | bytes 8388624 | tf_op jit(solution)/shard_map/all_gather | solution.py:152
  222.5 84.2 %conditional.1 = ((f32[256,4]{0,1:T(4,128)S(1)}, f32[256,4,128]{0,2,1:T(8,128)S(1)})) conditional(s32[]{:T(128)} %convert_element_type.61, (f32[256,4]{0,1:T(4,128)S(1)}, f32[256,4,128]{0,2,1:T(8,128)S(1)}) %tuple.12, (s32[32]{0:T(128)S(1)}, s32[256]{0:T(256)S(1)}, s32[256]{0:T(256)S(1)}, s32[32,32]{1,0:T(8,128)S(1)}, s32[32]{0:T(128)S(1)}, ...), branch_computations={%region_14.15_spmd, %region_15.19_spmd} | conditional | flops 4412816384 | bytes 163015328 | solution.py:169
  222.5 0.1 broadcast_bitcast_fusion
  222.6 0.2 select_reduce_fusion
  222.7 0.1 iota_compare_fusion
  222.9 6.9 %or_and_fusion = pred[256,8192]{0,1:T(8,128)(4,1)} fusion(s32[256]{0:T(256)S(1)} %get-tuple-element.44, s32[256]{0:T(256)S(1)} %get-tuple-element.43, s32[8192]{0:T(1024)S(1)} %bitcast.80, pred[8192]{0:T(1024)(128)(4,1)S(1)} %lt.18), kind=kLoop, calls=%fused_computation.10 | loop fusion | flops 8388608 | bytes 2140160 | tf_op jit(solution)/shard_map/cond/branch_1_fun/and | solution.py:95
  229.7 12.5 %reshape.259 = bf16[8192,4,128]{2,1,0:T(4,128)(2,1)} reshape(bf16[32,256,512]{2,1,0:T(8,128)(2,1)} %get-tuple-element.47) | data formatting | bytes 16777216 | tf_op jit(solution)/shard_map/cond/branch_1_fun/reshape | solution.py:88
  242.2 16.4 %fusion = (f32[256,4]{0,1:T(4,128)S(1)}, f32[4,8192,256]{2,1,0:T(8,128)}) fusion(pred[256,8192]{0,1:T(8,128)(4,1)} %or_and_fusion, bf16[256,4,128]{2,0,1:T(8,128)(2,1)S(1)} %get-tuple-element.48, bf16[8192,4,128]{2,1,0:T(4,128)(2,1)} %reshape.259), kind=kOutput, calls=%fused_computation.2 | convolution fusion | flops 2172648448 | bytes 44306432 | tf_op jit(solution)/shard_map/cond/branch_1_fun/rhe,khe->rhk/dot_general | solution.py:98
  258.6 15.1 %fusion.2 = f32[256,4]{0,1:T(4,128)S(1)} fusion(f32[4,8192,256]{2,1,0:T(8,128)} %get-tuple-element.120, f32[256,4]{0,1:T(4,128)S(1)} %get-tuple-element.119, pred[256,8192]{0,1:T(8,128)(4,1)} %or_and_fusion), kind=kLoop, calls=%fused_computation.4 | loop fusion | flops 41942016 | bytes 35659776 | tf_op jit(solution)/shard_map/cond/branch_1_fun/reduce_sum | solution.py:69
  273.8 12.5 %reshape.260 = bf16[8192,4,128]{2,1,0:T(4,128)(2,1)} reshape(bf16[32,256,512]{2,1,0:T(8,128)(2,1)} %get-tuple-element.50) | data formatting | bytes 16777216 | tf_op jit(solution)/shard_map/cond/branch_1_fun/reshape | solution.py:89
  286.3 1.0 copy.56
  287.3 19.1 %fusion.19 = f32[256,4,128]{2,0,1:T(8,128)S(1)} fusion(bf16[8192,4,128]{2,1,0:T(4,128)(2,1)} %reshape.260, f32[4,8192,256]{2,1,0:T(8,128)} %get-tuple-element.120, f32[256,4]{0,1:T(4,128)S(1)} %get-tuple-element.119, pred[256,8192]{0,1:T(8,128)(4,1)} %or_and_fusion, f32[256,4,128]{2,0,1:T(8,128)} %copy.56, f32[256,4]{0,1:T(4,128)S(1)} %get-tuple-element.118, ...), kind=kOutput, calls=%fused_computation.13 | convolution fusion | flops 2189819904 | bytes 45101056 | tf_op jit(solution)/shard_map/cond/branch_1_fun/rhk,khe->rhe/dot_general | solution.py:70
  306.4 0.2 copy.62
  306.7 3.4 convolution_convert_fusion.1
  310.1 0.0 all-reduce.3.cloned.1.call-update
  310.1 0.0 reduce-scatter.2.cloned.1.call-start
  310.1 0.0 copy-done.2
  310.2 39.3 %all-reduce.3.cloned.1.call-done = bf16[256,2048]{1,0:T(8,128)(2,1)} async-done(((bf16[256,2048]{1,0:T(8,128)(2,1)}), bf16[256,2048]{1,0:T(8,128)(2,1)}) %all-reduce.3.cloned.1.call-update) | async-done | bytes 1048592 | tf_op jit(solution)/shard_map/psum | solution.py:175
  349.5 1.1 fusion.41
  350.6 1.2 fusion.40
  351.8 1.1 stack.2
  352.9 107.6 %all_to_all.5 = bf16[32,64,2048]{2,1,0:T(8,128)(2,1)S(1)} all-to-all(bf16[32,64,2048]{2,1,0:T(8,128)(2,1)S(1)} %stack.2), channel_id=1, replica_groups=mesh['blk'=32,'head'=4] {'blk'}, dimensions={0} | all-to-all | bytes 16777216 | tf_op jit(solution)/shard_map/all_to_all | solution.py:13
  460.5 0.0 copy-done
  460.5 4.5 convolution_bitcast_fusion
  465.0 0.0 copy-done.7
  465.0 5.6 convolution_convert_fusion
  470.7 0.0 reduce-scatter.2.cloned.1.call-update
  470.7 205.3 %reduce-scatter.2.cloned.1.call-done = bf16[64,2048]{1,0:T(8,128)(2,1)} async-done(((bf16[2048,2048]{1,0:T(8,128)(2,1)}), bf16[64,2048]{1,0:T(8,128)(2,1)}) %reduce-scatter.2.cloned.1.call-update) | async-done | bytes 262160 | tf_op jit(solution)/shard_map/reduce_scatter | solution.py:185
  676.0 1.1 fusion.42
  677.1 1.8 fusion.45
  (22 shorter events, 0.2 us)
Async XLA Ops:
  6.5 454.0 %copy-start = (bf16[2,2048,256]{2,1,0:T(8,128)(2,1)S(1)}, bf16[2,2048,256]{2,1,0:T(8,128)(2,1)}, u32[]{:S(2)}) copy-start(bf16[2,2048,256]{2,1,0:T(8,128)(2,1)} %param.21) | copy-start | bytes 6291460
  6.5 10.2 %copy-start.1 = (s32[32,256]{1,0:T(8,128)S(1)}, s32[32,256]{1,0:T(8,128)}, u32[]{:S(2)}) copy-start(s32[32,256]{1,0:T(8,128)} %param.28) | copy-start | bytes 98308
  6.5 10.4 %copy-start.6 = (s32[28]{0:T(128)S(1)}, s32[28]{0:T(128)}, u32[]{:S(2)}) copy-start(s32[28]{0:T(128)} %param.27) | copy-start | bytes 340
  6.5 10.6 %copy-start.3 = (s32[32]{0:T(128)S(1)}, s32[32]{0:T(128)}, u32[]{:S(2)}) copy-start(s32[32]{0:T(128)} %param.25) | copy-start | bytes 388
  6.5 19.1 %copy-start.5 = (s32[32]{0:T(128)S(1)}, s32[32]{0:T(128)}, u32[]{:S(2)}) copy-start(s32[32]{0:T(128)} %param.26) | copy-start | bytes 388
  6.5 110.8 %all-gather.3.cloned.1.call-start = ((), (), s32[]{:S(2)}) async-start(), calls=%async_computation.2 | async-start | bytes 8650752 | tf_op jit(solution)/shard_map/all_gather | solution.py:151
  7.3 19.0 %copy-start.4 = (f32[2,512]{1,0:T(2,128)S(1)}, f32[2,512]{1,0:T(2,128)}, u32[]{:S(2)}) copy-start(f32[2,512]{1,0:T(2,128)} %param.18) | copy-start | bytes 12292
  7.3 215.2 %all-gather.5.cloned.1.call-start = ((), (), s32[]{:S(2)}) async-start(), calls=%async_computation.3 | async-start | bytes 8650752 | tf_op jit(solution)/shard_map/all_gather | solution.py:152
  8.0 341.4 %all-reduce.3.cloned.1.call-start = ((), (), s32[]{:S(2)}) async-start(), calls=%async_computation.4 | async-start | bytes 2097152 | tf_op jit(solution)/shard_map/psum | solution.py:175
  222.5 87.7 %copy-start.2 = (f32[2,2048]{1,0:T(2,128)S(1)}, f32[2,2048]{1,0:T(2,128)}, u32[]{:S(2)}) copy-start(f32[2,2048]{1,0:T(2,128)} %param.20) | copy-start | bytes 49156
  310.1 365.9 %reduce-scatter.2.cloned.1.call-start = ((), (), s32[]{:S(2)}) async-start(), calls=%async_computation.5 | async-start | bytes 8650752 | tf_op jit(solution)/shard_map/reduce_scatter | solution.py:185
  460.5 4.5 copy-start.7
Sparse Core Ops, SparseCore 0:
  10.5 106.7 all-gather.2
  120.4 101.9 all-gather.4
  310.2 39.2 all-reduce.2
  470.8 205.1 reduce-scatter.1
